TPU v7x, 32 devices: a whole 2x2x4 slice. The times are simulated.
32 devices in a mesh: ctx: 8 (over z, y), head: 4 (over x, core).
Axes of the slice: x: 2, y: 2, z: 4, core: 2. Of those that a mesh axis runs over, the one named last changes fastest.
Arguments:
- x_in: bfloat16 [4096, 8192], P('ctx', 'head'), may hold values from -6 to 6
- z_in: bfloat16 [4096, 8192], P('ctx', 'head'), may hold values from -6 to 6
- bc_in: bfloat16 [4096, 256], P('ctx', 'head'), may hold values from -6 to 6
- dt: float32 [4096, 128], P('ctx', 'head'), may hold values from 4.8828125e-05 to 0.25146484, as said below
- decay_scale: float32 [128], P('head'), may hold values from 0.5 to 2
- conv_x: bfloat16 [4, 8192], P(None, 'head'), may hold values from -3 to 3
- conv_bc: bfloat16 [4, 256], P(None, 'head'), may hold values from -3 to 3
- norm_gain: bfloat16 [8192], P('head'), may hold values from 0.25 to 1.75
- doc_start: int32 [4096], P('ctx'), may hold values from 0 to 1, as said below
Outputs:
- out: bfloat16 [4096, 8192], P('ctx', 'head')
Inputs may be any that keep to these rules, and one draw needn't show every extreme that they name: doc_start[0] = 0; going round the loop, two consecutive ones are at most 512 apart; the document that holds position 0 is exactly 512 long and begins 3 (4 - 1) or more positions before the end. `dt`: positive step sizes.
All inputs are finite; a program needn't handle non-finite values.
Results may differ from a plain program's by a relative error of at most 0.0034.
Values may be sent and summed in bfloat16 or wider, within the bound.
No kernel may reach another device: no remote copies, remote signals or barrier semaphores. Data moves between devices by JAX's collectives and lax.ppermute only.
A program may use at most 64 MiB of HBM per device.

v0:
```python
import jax
import jax.numpy as jnp
from jax import lax
from jax.sharding import PartitionSpec as P

HDIM = 64
DSTATE = 128
BLOCK = 256
CONV = 4


def shifted(value, axis, steps):
    count = lax.axis_size(axis)
    pairs = [(source, (source + steps) % count) for source in range(count)]
    return lax.ppermute(value, axis, pairs)


def causal_conv(padded, taps, same):
    rows = same.shape[1]
    total = jnp.zeros((rows, taps.shape[1]), jnp.float32)
    for offset in range(taps.shape[0]):
        piece = padded[offset : offset + rows].astype(jnp.float32) * taps[offset].astype(
            jnp.float32
        )
        total = total + jnp.where(same[offset][:, None], piece, 0.0)
    return jax.nn.silu(total)


def block_pass(state, values, bmat, cmat, steps, scale, doc_ids, doc_before):
    high = lax.Precision.HIGHEST
    log_decay = jnp.cumsum(-steps * scale[None, :], axis=0)
    scores = jnp.dot(cmat, bmat.T, precision=high)
    rows = doc_ids.shape[0]
    lower = jnp.arange(rows)[:, None] >= jnp.arange(rows)[None, :]
    keep = lower & (doc_ids[:, None] == doc_ids[None, :])
    decay_t = log_decay.T
    spread = decay_t[:, :, None] - decay_t[:, None, :]
    weights = (
        jnp.where(keep[None, :, :], jnp.exp(jnp.minimum(spread, 0.0)), 0.0) * scores[None, :, :]
    )
    output = jnp.einsum("hts,shp->htp", weights, values, precision=high)
    live = doc_ids == doc_before
    carried = jnp.einsum("tn,hpn->htp", cmat, state, precision=high)
    output = output + jnp.where(live[None, :, None], jnp.exp(decay_t)[:, :, None] * carried, 0.0)
    tail = doc_ids == doc_ids[-1]
    to_end = jnp.where(tail[:, None], jnp.exp(log_decay[-1][None, :] - log_decay), 0.0)
    fresh = jnp.einsum("sh,shp,sn->hpn", to_end, values, bmat, precision=high)
    keep_state = jnp.where(doc_ids[-1] == doc_before, jnp.exp(log_decay[-1]), 0.0)
    return (keep_state[:, None, None] * state + fresh, output)


def gated_norm(output, gate, gain):
    rows, heads, width = output.shape
    mixed = output * jax.nn.silu(gate.astype(jnp.float32)).reshape(rows, heads, width)
    factor = lax.rsqrt(jnp.mean(mixed * mixed, axis=-1, keepdims=True) + 1e-05)
    normed = mixed * factor * gain.astype(jnp.float32).reshape(heads, width)
    return normed.reshape(rows, heads * width).astype(jnp.bfloat16)


def on_device(x_in, z_in, bc_in, dt, decay_scale, conv_x, conv_bc, norm_gain, doc_start):
    high = lax.Precision.HIGHEST
    positions = x_in.shape[0]
    local_heads = dt.shape[1]
    lead = CONV - 1
    doc_ids = jnp.cumsum(doc_start)
    in_last = (doc_ids[-lead:] == doc_ids[-1])[:, None]
    tail_x = jnp.where(in_last, x_in[-lead:], jnp.zeros_like(x_in[-lead:]))
    tail_bc = jnp.where(in_last, bc_in[-lead:], jnp.zeros_like(bc_in[-lead:]))
    rim_x, rim_bc = shifted((tail_x, tail_bc), "ctx", 1)
    x_pad = jnp.concatenate([rim_x, x_in], axis=0)
    bc_pad = jnp.concatenate([rim_bc, bc_in], axis=0)
    ids_pad = jnp.concatenate([jnp.zeros((lead,), jnp.int32), doc_ids], axis=0)
    same = jnp.stack([ids_pad[offset : offset + positions] == doc_ids for offset in range(CONV)])
    x_conv = causal_conv(x_pad, conv_x, same)
    bc_local = causal_conv(bc_pad, conv_bc, same).astype(jnp.bfloat16)
    bc_whole = lax.all_gather(bc_local, "head", axis=1, tiled=True).astype(jnp.float32)
    bmat = bc_whole[:, :DSTATE]
    cmat = bc_whole[:, DSTATE:]
    blocks = positions // BLOCK
    empty = jnp.zeros((local_heads, HDIM, DSTATE), jnp.float32)
    end_state = empty
    pieces = []
    for index in range(blocks):
        low = index * BLOCK
        high_end = low + BLOCK
        before = jnp.full((), -1, jnp.int32) if index == 0 else doc_ids[low - 1]
        block_values = x_conv[low:high_end].reshape(BLOCK, local_heads, HDIM)
        end_state, block_out = block_pass(
            end_state,
            block_values,
            bmat[low:high_end],
            cmat[low:high_end],
            dt[low:high_end],
            decay_scale,
            doc_ids[low:high_end],
            before,
        )
        pieces.append(block_out)
    output = jnp.concatenate(pieces, axis=1)
    device_decay = jnp.cumsum(-dt * decay_scale[None, :], axis=0)
    through = jnp.where(doc_ids[-1] == 0, jnp.exp(device_decay[-1]), 0.0)

    def relay_turn(turn, incoming):
        return shifted(through[:, None, None] * incoming + end_state, "ctx", 1)

    state_in = lax.fori_loop(0, lax.axis_size("ctx") // 8, relay_turn, empty)
    carried = jnp.einsum("tn,hpn->htp", cmat, state_in, precision=high)
    live = (doc_ids == 0)[None, :, None]
    output = output + jnp.where(live, jnp.exp(device_decay.T)[:, :, None] * carried, 0.0)
    return gated_norm(jnp.transpose(output, (1, 0, 2)), z_in, norm_gain)


def solution(mesh):
    in_specs = (
        P("ctx", "head"),
        P("ctx", "head"),
        P("ctx", "head"),
        P("ctx", "head"),
        P("head"),
        P(None, "head"),
        P(None, "head"),
        P("head"),
        P("ctx"),
    )
    out_specs = P("ctx", "head")
    return jax.shard_map(
        on_device, mesh=mesh, in_specs=in_specs, out_specs=out_specs, check_vma=False
    )
```

profile of v0, /device:TPU:0, one launch (start us, length us, event | category | flops | bytes accessed | tf_op | source)
XLA Modules:
  0.0 98.0 jit_solution(13949360632276049648)
XLA Ops:
  0.0 1.0 %reduce-window.29 = s32[4,128]{1,0:T(4,128)S(1)} reduce-window(s32[4,128]{1,0:T(4,128)} %bitcast.145, s32[]{:T(128)} %constant.12.clone.1), window={size=1x128 pad=0_0x127_0}, to_apply=%region_0.0 | reduce-window | flops 65024 | bytes 4100 | tf_op jit(solution)/shard_map/reduce-window
  3.1 0.8 slice_select_fusion.1
  3.9 3.0 %collective-permute-start = (bf16[3,64]{0,1:T(8,128)(2,1)S(1)}, bf16[3,64]{0,1:T(8,128)(2,1)S(1)}, u32[]{:S(2)}, u32[]{:S(2)}) collective-permute-start(bf16[3,64]{0,1:T(8,128)(2,1)S(1)} %slice_select_fusion.1), channel_id=1, source_target_pairs={{0,4},{4,8},{8,12},{12,16},{16,20},{20,24},{24,28},{28,0},{1,5},{5... | collective-permute-start | bytes 1160 | tf_op jit(solution)/shard_map/ppermute | solution.py:15
  6.9 0.8 slice_select_fusion
  7.7 1.6 %collective-permute-start.1 = (bf16[3,2048]{1,0:T(4,128)(2,1)S(1)}, bf16[3,2048]{1,0:T(4,128)(2,1)S(1)}, u32[]{:S(2)}, u32[]{:S(2)}) collective-permute-start(bf16[3,2048]{1,0:T(4,128)(2,1)S(1)} %slice_select_fusion), channel_id=1, source_target_pairs={{0,4},{4,8},{8,12},{12,16},{16,20},{20,24},{24,28},{28,0},{1,5},{5... | collective-permute-start | bytes 36872 | tf_op jit(solution)/shard_map/ppermute | solution.py:15
  10.6 0.8 fusion.50
  11.4 0.8 multiply_bitcast_fusion.1
  15.1 0.9 copy_bitcast_fusion
  18.1 1.1 %reduce-window.39 = f32[32,4,128]{2,0,1:T(8,128)S(1)} reduce-window(f32[32,4,128]{2,0,1:T(8,128)S(1)} %copy_bitcast_fusion, f32[]{:T(128)} %constant.13.clone.1), window={size=1x1x128 pad=0_0x0_0x127_0}, to_apply=%region_6.7 | reduce-window | flops 2080768 | bytes 131076 | tf_op jit(solution)/shard_map/reduce-window.6
  19.7 0.8 bitcast_convert_fusion.3
  21.7 2.5 %broadcast_compare_fusion.1 = (pred[256]{0:T(512)(128)(4,1)S(1)}, pred[256]{0:T(512)(128)(4,1)}, pred[256]{0:T(512)(128)(4,1)S(1)}, pred[256]{0:T(512)(128)(4,1)}) fusion(s32[]{:T(128)} %bitcast.27, s32[4,128]{1,0:T(4,128)S(1)} %get-tuple-element.16, s32[]{:T(128)} %bitcast.19, s32[]{:T(128)} %bitcast.20), kind=kLoop, calls=%fused_computation.127 | loop fusion | flops 1024 | bytes 3084 | tf_op jit(solution)/shard_map/eq | solution.py:45
  24.4 0.9 slice_convert_fusion.3
  27.4 4.7 %convert_multiply_fusion = f32[512,2048]{1,0:T(8,128)} fusion(bf16[512,2048]{1,0:T(8,128)(2,1)} %param.10), kind=kLoop, calls=%fused_computation.12 | loop fusion | flops 5242880 | bytes 6291456 | tf_op jit(solution)/shard_map/jit(silu)/mul | solution.py:54
  32.0 0.8 fusion.71
  32.8 5.5 %copy.68 = f32[512,2048]{0,1:T(8,128)} copy(f32[512,2048]{1,0:T(8,128)} %convert_multiply_fusion) | data formatting | bytes 8388608 | tf_op jit(solution)/shard_map/jit(silu)/mul | solution.py:54
  38.6 5.8 %all_gather.3 = bf16[512,256]{0,1:T(8,128)(2,1)S(1)} all-gather(bf16[512,64]{0,1:T(8,128)(2,1)S(1)} %multiply_convert_fusion.1), channel_id=1, replica_groups=mesh['ctx'=8,'head'=4] {'head'}, dimensions={1}, use_global_device_ids=true | all-gather | bytes 327680 | tf_op jit(solution)/shard_map/all_gather | solution.py:76
  44.4 0.9 fusion.59
  45.3 2.3 %fusion.48 = f32[32,64,256]{2,1,0:T(8,128)} fusion(bf16[512,256]{0,1:T(8,128)(2,1)S(1)} %all_gather.3), kind=kOutput, calls=%fused_computation.49 | convolution fusion | flops 805306368 | bytes 2162688 | tf_op jit(solution)/shard_map/tn,hpn->htp/dot_general | solution.py:43
  47.6 0.9 fusion.64
  48.5 4.2 %divide_multiply_fusion = f32[512,2048]{1,0:T(8,128)S(1)} fusion(bf16[512,2048]{1,0:T(8,128)(2,1)S(1)} %copy-done.3, bf16[3,2048]{1,0:T(4,128)(2,1)S(1)} %collective-permute-done.1, f32[2048]{0:T(1024)S(1)} %bitcast.143, f32[2048]{0:T(1024)S(1)} %bitcast.144, f32[2048]{0:T(1024)S(1)} %bitcast.142, f32[2048]{0:T(1024)S(1)} %bitcast.141, ...), kind=kLoop, calls=%fused_computation.25 | loop fusion | flops 28311552 | bytes 6338048 | tf_op jit(solution)/shard_map/jit(silu)/mul | solution.py:26
  52.7 2.3 %fusion.83 = (f32[256,2048]{1,0:T(8,128)}, f32[256,2048]{1,0:T(8,128)}) fusion(f32[512,2048]{1,0:T(8,128)S(1)} %divide_multiply_fusion), kind=kLoop, calls=%fused_computation.139 | loop fusion | bytes 8388608 | tf_op jit(solution)/shard_map/slice | solution.py:87
  55.0 1.9 %copy.59 = f32[256,2048]{0,1:T(8,128)S(1)} copy(f32[256,2048]{1,0:T(8,128)} %get-tuple-element.20) | data formatting | bytes 4194304 | tf_op jit(solution)/shard_map/slice | solution.py:87
  56.9 1.7 %fusion.37 = f32[32,64,128]{2,1,0:T(8,128)S(1)} fusion(f32[256,32,64]{0,2,1:T(8,128)S(1)} %bitcast.136, f32[256,32]{0,1:T(8,128)S(1)} %exponential_select_fusion.1, f32[32]{0:T(128)} %fusion.75, bf16[512,256]{0,1:T(8,128)(2,1)S(1)} %all_gather.3), kind=kOutput, calls=%fused_computation.44 | convolution fusion | flops 806092800 | bytes 3244160 | tf_op jit(solution)/shard_map/sh,shp,sn->hpn/dot_general | solution.py:47
  58.7 2.4 %fusion.55 = f32[32,64,256]{2,1,0:T(8,128)} fusion(f32[32,64,128]{2,1,0:T(8,128)S(1)} %fusion.37, bf16[512,256]{0,1:T(8,128)(2,1)S(1)} %all_gather.3), kind=kOutput, calls=%fused_computation.68 | convolution fusion | flops 805306368 | bytes 3211264 | tf_op jit(solution)/shard_map/tn,hpn->htp/dot_general | solution.py:43
  61.0 1.9 %copy.64 = f32[256,2048]{0,1:T(8,128)S(1)} copy(f32[256,2048]{1,0:T(8,128)} %get-tuple-element.18) | data formatting | bytes 4194304 | tf_op jit(solution)/shard_map/slice | solution.py:87
  63.0 1.1 %fusion.43 = f32[32,64,128]{2,1,0:T(8,128)S(1)} fusion(f32[256,32,64]{0,2,1:T(8,128)S(1)} %bitcast.134, f32[256,32]{0,1:T(8,128)S(1)} %exponential_select_fusion, f32[32,64,128]{2,1,0:T(8,128)S(1)} %fusion.37, f32[32]{0:T(128)S(1)} %copy-done.18, f32[32]{0:T(128)S(1)} %copy-done.17, bf16[512,256]{0,1:T(8,128)(2,1)S(1)} %all_gather.3), kind=kOutput, calls=%fused_computation.46 | convolution fusion | flops 806617088 | bytes 4293632 | tf_op jit(solution)/shard_map/sh,shp,sn->hpn/dot_general | solution.py:47
  64.2 1.8 %collective-permute-start.2 = (f32[32,64,128]{2,1,0:T(8,128)S(1)}, f32[32,64,128]{2,1,0:T(8,128)S(1)}, u32[]{:S(2)}, u32[]{:S(2)}) collective-permute-start(f32[32,64,128]{2,1,0:T(8,128)S(1)} %fusion.43), channel_id=1, source_target_pairs={{0,4},{4,8},{8,12},{12,16},{16,20},{20,24},{24,28},{28,0},{1,5},{5... | collective-permute-start | bytes 3145736 | tf_op jit(solution)/shard_map/while/body/eval_jaxpr/ppermute | solution.py:15
  66.0 10.0 %bitcast_add_fusion = f32[32,256,64]{1,2,0:T(8,128)S(1)} fusion(f32[32,64,256]{2,1,0:T(8,128)S(1)} %copy-done.5, f32[256,32,64]{0,2,1:T(8,128)S(1)} %bitcast.135, f32[256,256]{1,0:T(8,128)S(1)} %copy-done.7, f32[32,256]{1,0:T(8,128)S(1)} %copy-done.11, pred[256,256]{1,0:T(8,128)(4,1)S(1)} %copy-done.10, f32[32,256]{1,0:T(8,128)S(1)} %copy-done.13, ...), kind=kOutput, calls=%fused_computation.38 | convolution fusion | flops 1620574208 | bytes 6684928 | tf_op jit(solution)/shard_map/hts,shp->htp/dot_general | solution.py:41
  76.1 10.2 %bitcast_add_fusion.1 = f32[32,256,64]{1,2,0:T(8,128)S(1)} fusion(f32[32,64,256]{2,1,0:T(8,128)S(1)} %copy-done.4, f32[256,32,64]{0,2,1:T(8,128)S(1)} %bitcast.137, f32[256,256]{1,0:T(8,128)S(1)} %copy-done.6, f32[32,256]{1,0:T(8,128)S(1)} %copy-done.12, pred[256,256]{1,0:T(8,128)(4,1)S(1)} %copy-done.9, f32[32,256]{1,0:T(8,128)S(1)} %copy-done.14, ...), kind=kOutput, calls=%fused_computation.39 | convolution fusion | flops 1620574208 | bytes 6684928 | tf_op jit(solution)/shard_map/hts,shp->htp/dot_general | solution.py:41
  86.3 6.2 %collective-permute-done.2 = f32[32,64,128]{2,1,0:T(8,128)S(1)} collective-permute-done((f32[32,64,128]{2,1,0:T(8,128)S(1)}, f32[32,64,128]{2,1,0:T(8,128)S(1)}, u32[]{:S(2)}, u32[]{:S(2)}) %collective-permute-start.2) | collective-permute-done | bytes 1048608 | tf_op jit(solution)/shard_map/while/body/eval_jaxpr/ppermute | solution.py:15
  92.5 2.5 %multiply_reduce_fusion = (f32[512,32]{0,1:T(8,128)S(1)}, f32[512,32,64]{0,2,1:T(8,128)S(1)}) fusion(f32[512,32,64]{0,2,1:T(8,128)S(1)} %bitcast.132, f32[32,64,128]{2,1,0:T(8,128)S(1)} %collective-permute-done.2, bf16[512,256]{0,1:T(8,128)(2,1)S(1)} %all_gather.3, f32[32,512]{1,0:T(8,128)S(1)} %bitcast_exponential_fusion, ...), kind=kOutput, calls=%fused_computation.21 | convolution fusion | flops 1617936384 | bytes 13894144 | tf_op jit(solution)/shard_map/tn,hpn->htp/dot_general | solution.py:107
  95.6 2.4 %copy.69 = bf16[512,2048]{1,0:T(8,128)(2,1)} copy(bf16[512,2048]{0,1:T(8,128)(2,1)S(1)} %bitcast.133) | data formatting | bytes 4194304 | tf_op jit(solution)/shard_map/convert_element_type | solution.py:57
  (82 shorter events, 10.6 us)
Async XLA Ops:
  3.9 34.5 %collective-permute-start = (bf16[3,64]{0,1:T(8,128)(2,1)S(1)}, bf16[3,64]{0,1:T(8,128)(2,1)S(1)}, u32[]{:S(2)}, u32[]{:S(2)}) collective-permute-start(bf16[3,64]{0,1:T(8,128)(2,1)S(1)} %slice_select_fusion.1), channel_id=1, source_target_pairs={{0,4},{4,8},{8,12},{12,16},{16,20},{20,24},{24,28},{28,0},{1,5},{5... | collective-permute-start | bytes 1160 | tf_op jit(solution)/shard_map/ppermute | solution.py:15
  7.7 40.8 %collective-permute-start.1 = (bf16[3,2048]{1,0:T(4,128)(2,1)S(1)}, bf16[3,2048]{1,0:T(4,128)(2,1)S(1)}, u32[]{:S(2)}, u32[]{:S(2)}) collective-permute-start(bf16[3,2048]{1,0:T(4,128)(2,1)S(1)} %slice_select_fusion), channel_id=1, source_target_pairs={{0,4},{4,8},{8,12},{12,16},{16,20},{20,24},{24,28},{28,0},{1,5},{5... | collective-permute-start | bytes 36872 | tf_op jit(solution)/shard_map/ppermute | solution.py:15
  32.8 5.5 %copy-start.15 = (bf16[2048]{0:T(1024)(128)(2,1)S(1)}, bf16[2048]{0:T(1024)(128)(2,1)}, u32[]{:S(2)}) copy-start(bf16[2048]{0:T(1024)(128)(2,1)} %param.16) | copy-start | bytes 12292
  32.8 5.6 %copy-start.8 = (bf16[512,64]{0,1:T(8,128)(2,1)S(1)}, bf16[512,64]{0,1:T(8,128)(2,1)}, u32[]{:S(2)}) copy-start(bf16[512,64]{0,1:T(8,128)(2,1)} %param.11) | copy-start | bytes 196612
  32.8 15.7 %copy-start.3 = (bf16[512,2048]{1,0:T(8,128)(2,1)S(1)}, bf16[512,2048]{1,0:T(8,128)(2,1)}, u32[]{:S(2)}) copy-start(bf16[512,2048]{1,0:T(8,128)(2,1)} %param.9) | copy-start | bytes 6291460
  56.9 4.1 %copy-start.1 = (f32[256,2048]{0,1:T(8,128)}, f32[256,2048]{0,1:T(8,128)S(1)}, u32[]{:S(2)}) copy-start(f32[256,2048]{0,1:T(8,128)S(1)} %copy.59) | copy-start | bytes 6291460
  58.6 4.4 %copy-start.17 = (f32[32]{0:T(128)S(1)}, f32[32]{0:T(128)}, u32[]{:S(2)}) copy-start(f32[32]{0:T(128)} %fusion.71) | copy-start | bytes 388
  58.7 4.4 %copy-start.18 = (f32[32]{0:T(128)S(1)}, f32[32]{0:T(128)}, u32[]{:S(2)}) copy-start(f32[32]{0:T(128)} %broadcast_select_fusion) | copy-start | bytes 388
  63.0 3.0 %copy-start.5 = (f32[32,64,256]{2,1,0:T(8,128)S(1)}, f32[32,64,256]{2,1,0:T(8,128)}, u32[]{:S(2)}) copy-start(f32[32,64,256]{2,1,0:T(8,128)} %fusion.55) | copy-start | bytes 6291460
  63.0 3.0 %copy-start.7 = (f32[256,256]{1,0:T(8,128)S(1)}, f32[256,256]{1,0:T(8,128)}, u32[]{:S(2)}) copy-start(f32[256,256]{1,0:T(8,128)} %fusion.59) | copy-start | bytes 786436
  63.0 2.9 %copy-start.10 = (pred[256,256]{1,0:T(8,128)(4,1)S(1)}, pred[256,256]{1,0:T(8,128)(4,1)}, u32[]{:S(2)}) copy-start(pred[256,256]{1,0:T(8,128)(4,1)} %get-tuple-element.50) | copy-start | bytes 196612
  63.0 2.9 %copy-start.11 = (f32[32,256]{1,0:T(8,128)S(1)}, f32[32,256]{1,0:T(8,128)}, u32[]{:S(2)}) copy-start(f32[32,256]{1,0:T(8,128)} %get-tuple-element.24) | copy-start | bytes 98308
  63.0 2.9 %copy-start.13 = (f32[32,256]{1,0:T(8,128)S(1)}, f32[32,256]{1,0:T(8,128)}, u32[]{:S(2)}) copy-start(f32[32,256]{1,0:T(8,128)} %fusion.81) | copy-start | bytes 98308
  63.0 2.9 %copy-start.20 = (pred[256]{0:T(512)(128)(4,1)S(1)}, pred[256]{0:T(512)(128)(4,1)}, u32[]{:S(2)}) copy-start(pred[256]{0:T(512)(128)(4,1)} %get-tuple-element.32) | copy-start | bytes 772
  64.2 28.3 %collective-permute-start.2 = (f32[32,64,128]{2,1,0:T(8,128)S(1)}, f32[32,64,128]{2,1,0:T(8,128)S(1)}, u32[]{:S(2)}, u32[]{:S(2)}) collective-permute-start(f32[32,64,128]{2,1,0:T(8,128)S(1)} %fusion.43), channel_id=1, source_target_pairs={{0,4},{4,8},{8,12},{12,16},{16,20},{20,24},{24,28},{28,0},{1,5},{5... | collective-permute-start | bytes 3145736 | tf_op jit(solution)/shard_map/while/body/eval_jaxpr/ppermute | solution.py:15
  66.0 10.0 %copy-start.2 = (f32[256,2048]{0,1:T(8,128)S(1)}, f32[256,2048]{0,1:T(8,128)}, u32[]{:S(2)}) copy-start(f32[256,2048]{0,1:T(8,128)} %copy-done.1) | copy-start | bytes 6291460
  66.0 10.0 %copy-start.4 = (f32[32,64,256]{2,1,0:T(8,128)S(1)}, f32[32,64,256]{2,1,0:T(8,128)}, u32[]{:S(2)}) copy-start(f32[32,64,256]{2,1,0:T(8,128)} %fusion.48) | copy-start | bytes 6291460
  66.0 10.0 %copy-start.6 = (f32[256,256]{1,0:T(8,128)S(1)}, f32[256,256]{1,0:T(8,128)}, u32[]{:S(2)}) copy-start(f32[256,256]{1,0:T(8,128)} %fusion.64) | copy-start | bytes 786436
  66.0 10.0 %copy-start.9 = (pred[256,256]{1,0:T(8,128)(4,1)S(1)}, pred[256,256]{1,0:T(8,128)(4,1)}, u32[]{:S(2)}) copy-start(pred[256,256]{1,0:T(8,128)(4,1)} %get-tuple-element.51) | copy-start | bytes 196612
  66.0 10.0 %copy-start.12 = (f32[32,256]{1,0:T(8,128)S(1)}, f32[32,256]{1,0:T(8,128)}, u32[]{:S(2)}) copy-start(f32[32,256]{1,0:T(8,128)} %get-tuple-element.25) | copy-start | bytes 98308
  66.0 10.0 %copy-start.14 = (f32[32,256]{1,0:T(8,128)S(1)}, f32[32,256]{1,0:T(8,128)}, u32[]{:S(2)}) copy-start(f32[32,256]{1,0:T(8,128)} %fusion.79) | copy-start | bytes 98308
  66.0 10.0 %copy-start.19 = (pred[256]{0:T(512)(128)(4,1)S(1)}, pred[256]{0:T(512)(128)(4,1)}, u32[]{:S(2)}) copy-start(pred[256]{0:T(512)(128)(4,1)} %get-tuple-element.34) | copy-start | bytes 772
  76.1 16.5 %copy-start = (f32[512,2048]{0,1:T(8,128)S(1)}, f32[512,2048]{0,1:T(8,128)}, u32[]{:S(2)}) copy-start(f32[512,2048]{0,1:T(8,128)} %copy.68) | copy-start | bytes 12582916
  76.1 16.5 %copy-start.16 = (pred[512]{0:T(512)(128)(4,1)S(1)}, pred[512]{0:T(512)(128)(4,1)}, u32[]{:S(2)}) copy-start(pred[512]{0:T(512)(128)(4,1)} %get-tuple-element.11) | copy-start | bytes 1540
where the time goes:
time: 98.6 us; the launch traced here: 98 us
  matrix products  32 us (32%)
  other arithmetic  27.6 us (28%)
  local copies, waits for them, and re-layouts  17.1 us (17%)
  starting transfers between devices  6.29 us (6%)
  waiting for transfers between devices  6.22 us (6%)
  blocking collectives  5.79 us (6%)
  between operations  2.89 us (3%)
    dot_general x2, matrix products, block_pass(): output = jnp.einsum('hts,shp->htp', weights, values, precision=high)  20.2 us
    ppermute x3, starting transfers between devices, shifted(): return lax.ppermute(value, axis, pairs)  6.29 us
    ppermute x3, waiting for transfers between devices, shifted(): return lax.ppermute(value, axis, pairs)  6.22 us
    slice x3, local copies, waits for them, and re-layouts, on_device(): block_values = x_conv[low:high_end].reshape(BLOCK, local_heads, HDIM)  6.14 us
    another operation x12, other arithmetic  5.84 us
    all_gather x1, blocking collectives, on_device(): lax.all_gather(bc_local, 'head', axis=1, tiled=True).astype(jnp.float32)  5.79 us
    mul x1, local copies, waits for them, and re-layouts, gated_norm(): jax.nn.silu(gate.astype(jnp.float32)).reshape(rows, heads, width)  5.5 us
    dot_general x2, matrix products, block_pass(): carried = jnp.einsum('tn,hpn->htp', cmat, state, precision=high)  4.66 us
  transfers between devices with their start and end apart: 3, of which 1 were waited for; matrix products, arithmetic and copies ran while one was open for 53% of the time, Pallas kernels for 0%

commit v1 on v0

--- a/solution.py
+++ b/solution.py
@@ -7,6 +7,19 @@
 DSTATE = 128
 BLOCK = 256
 CONV = 4
+
+
+def ring_gather(x, axis, dim):
+    ways = lax.axis_size(axis)
+    up = [(d, (d + 1) % ways) for d in range(ways)]
+    down = [(d, (d - 1) % ways) for d in range(ways)]
+    earlier, later = ([x], [x])
+    for _ in range(ways // 2):
+        earlier.append(lax.ppermute(earlier[-1], axis, up))
+    for _ in range((ways - 1) // 2):
+        later.append(lax.ppermute(later[-1], axis, down))
+    line = jnp.concatenate([*earlier[::-1], *later[1:]], axis=dim)
+    return jnp.roll(line, (lax.axis_index(axis) - ways // 2) * x.shape[dim], axis=dim)
 
 
 def shifted(value, axis, steps):
@@ -73,7 +86,7 @@
     same = jnp.stack([ids_pad[offset : offset + positions] == doc_ids for offset in range(CONV)])
     x_conv = causal_conv(x_pad, conv_x, same)
     bc_local = causal_conv(bc_pad, conv_bc, same).astype(jnp.bfloat16)
-    bc_whole = lax.all_gather(bc_local, "head", axis=1, tiled=True).astype(jnp.float32)
+    bc_whole = ring_gather(bc_local, "head", 1).astype(jnp.float32)
     bmat = bc_whole[:, :DSTATE]
     cmat = bc_whole[:, DSTATE:]
     blocks = positions // BLOCK

time: 98.6 us -> 86.3 us (0.88)
  blocking collectives: 5.79 us -> 0 us
  other arithmetic: 27.6 us -> 23.9 us
  matrix products: 32 us -> 29.3 us
  waiting for transfers between devices: 6.22 us -> 3.74 us
  starting transfers between devices: 6.29 us -> 8.14 us
    all_gather x1 -> x0, blocking collectives: 5.79 us -> none  [on_device(): lax.all_gather(bc_local, 'head', axis=1, tiled=True).astype(jnp.float32)]
    dot_general x2, matrix products: 4.66 us -> 2.15 us  [block_pass(): carried = jnp.einsum('tn,hpn->htp', cmat, state, precision=high)]
    ppermute x3, waiting for transfers between devices: 6.22 us -> 3.73 us  [shifted(): return lax.ppermute(value, axis, pairs)]
    ppermute x0 -> x3, starting transfers between devices: none -> 1.85 us  [the longest x1 1.73 us: ring_gather(): later.append(lax.ppermute(later[-1], axis, down))]
    dot_general x2, matrix products: 1.85 us -> 0.54 us  [block_pass(): scores = jnp.dot(cmat, bmat.T, precision=high)]
    another operation x12, other arithmetic: 5.84 us -> 4.61 us
    exp x2, other arithmetic: 1.37 us -> 0.19 us  [block_pass(): jnp.exp(decay_t)[:, :, None] * carried]
  transfers between devices with their start and end apart: 3 -> 6, of which waited for: 1 -> 1; matrix products, arithmetic and copies ran while one was open for 53% -> 67% of each run, Pallas kernels for 0% -> 0%
where the time goes in v1:
time: 86.3 us; the launch traced here: 85.7 us
  matrix products  29.3 us (34%)
  other arithmetic  23.9 us (28%)
  local copies, waits for them, and re-layouts  17.8 us (21%)
  starting transfers between devices  8.14 us (9%)
  waiting for transfers between devices  3.74 us (4%)
  between operations  2.85 us (3%)
    dot_general x2, matrix products, block_pass(): output = jnp.einsum('hts,shp->htp', weights, values, precision=high)  20.1 us
    ppermute x3, starting transfers between devices, shifted(): return lax.ppermute(value, axis, pairs)  6.3 us
    mul x1, local copies, waits for them, and re-layouts, gated_norm(): jax.nn.silu(gate.astype(jnp.float32)).reshape(rows, heads, width)  5.5 us
    slice x3, local copies, waits for them, and re-layouts, on_device(): block_values = x_conv[low:high_end].reshape(BLOCK, local_heads, HDIM)  5.48 us
    mul x1, other arithmetic, gated_norm(): jax.nn.silu(gate.astype(jnp.float32)).reshape(rows, heads, width)  4.66 us
    another operation x12, other arithmetic  4.61 us
    mul x1, other arithmetic, causal_conv(): return jax.nn.silu(total)  4.17 us
    dot_general x2, matrix products, block_pass(): fresh = jnp.einsum('sh,shp,sn->hpn', to_end, values, bmat, precision=high)  3.79 us
  transfers between devices with their start and end apart: 6, of which 1 were waited for; matrix products, arithmetic and copies ran while one was open for 67% of the time, Pallas kernels for 0%

profile of v1, /device:TPU:0, one launch (start us, length us, event | category | flops | bytes accessed | tf_op | source)
XLA Modules:
  0.0 85.7 jit_solution(3680445581704680923)
XLA Ops:
  0.0 1.0 %reduce-window.29 = s32[4,128]{1,0:T(4,128)S(1)} reduce-window(s32[4,128]{1,0:T(4,128)} %bitcast.142, s32[]{:T(128)} %constant.37.clone.1), window={size=1x128 pad=0_0x127_0}, to_apply=%region_0.0 | reduce-window | flops 65024 | bytes 4100 | tf_op jit(solution)/shard_map/reduce-window
  1.8 0.6 fusion.80
  2.4 0.7 slice_compare_fusion
  3.1 1.0 %copy.44 = bf16[512,64]{1,0:T(8,128)(2,1)S(1)} copy(bf16[512,64]{0,1:T(8,128)(2,1)} %param.11) | data formatting | bytes 131072 | tf_op args[2]
  4.1 3.0 %collective-permute-start = (bf16[3,64]{1,0:T(4,128)(2,1)S(1)}, bf16[3,64]{1,0:T(4,128)(2,1)S(1)}, u32[]{:S(2)}, u32[]{:S(2)}) collective-permute-start(bf16[3,64]{1,0:T(4,128)(2,1)S(1)} %slice_select_fusion.1), channel_id=1, source_target_pairs={{0,4},{4,8},{8,12},{12,16},{16,20},{20,24},{24,28},{28,0},{1,5},{5... | collective-permute-start | bytes 1160 | tf_op jit(solution)/shard_map/ppermute | solution.py:28
  7.1 0.8 slice_select_fusion
  7.9 1.6 %collective-permute-start.4 = (bf16[3,2048]{1,0:T(4,128)(2,1)S(1)}, bf16[3,2048]{1,0:T(4,128)(2,1)S(1)}, u32[]{:S(2)}, u32[]{:S(2)}) collective-permute-start(bf16[3,2048]{1,0:T(4,128)(2,1)S(1)} %slice_select_fusion), channel_id=1, source_target_pairs={{0,4},{4,8},{8,12},{12,16},{16,20},{20,24},{24,28},{28,0},{1,5},{5... | collective-permute-start | bytes 36872 | tf_op jit(solution)/shard_map/ppermute | solution.py:28
  9.6 0.7 slice.189
  11.0 0.8 multiply_bitcast_fusion.2
  13.5 0.9 %copy_bitcast_fusion = f32[32,4,128]{2,0,1:T(8,128)S(1)} fusion(f32[512,32]{0,1:T(8,128)} %param.12, f32[32]{0:T(128)} %param.13), kind=kLoop, calls=%fused_computation.61 | loop fusion | flops 32768 | bytes 131200 | tf_op jit(solution)/shard_map/reshape.13
  15.3 1.2 %reduce-window.39 = f32[32,4,128]{2,0,1:T(8,128)S(1)} reduce-window(f32[32,4,128]{2,0,1:T(8,128)S(1)} %copy_bitcast_fusion, f32[]{:T(128)} %constant.39.clone.1), window={size=1x1x128 pad=0_0x0_0x127_0}, to_apply=%region_6.7 | reduce-window | flops 2080768 | bytes 131076 | tf_op jit(solution)/shard_map/reduce-window.6
  16.9 0.8 bitcast_convert_fusion.3
  17.7 0.9 %slice_convert_fusion.3 = (f32[1,2048]{1,0:T(1,128)S(1)}, f32[1,2048]{1,0:T(1,128)S(1)}, f32[1,2048]{1,0:T(1,128)S(1)}, f32[1,2048]{1,0:T(1,128)S(1)}) fusion(bf16[4,2048]{1,0:T(4,128)(2,1)} %param.14), kind=kLoop, calls=%fused_computation.102 | loop fusion | flops 8192 | bytes 49152 | tf_op jit(solution)/shard_map/mul | solution.py:35
  19.8 2.4 %broadcast_compare_fusion.1 = (pred[256]{0:T(512)(128)(4,1)S(1)}, pred[256]{0:T(512)(128)(4,1)}, pred[256]{0:T(512)(128)(4,1)S(1)}, pred[256]{0:T(512)(128)(4,1)}) fusion(s32[]{:T(128)} %bitcast.27, s32[4,128]{1,0:T(4,128)S(1)} %get-tuple-element.16, s32[]{:T(128)} %bitcast.19, s32[]{:T(128)} %bitcast.20), kind=kLoop, calls=%fused_computation.126 | loop fusion | flops 1024 | bytes 3084 | tf_op jit(solution)/shard_map/eq | solution.py:58
  24.5 4.7 %convert_multiply_fusion = f32[512,2048]{1,0:T(8,128)} fusion(bf16[512,2048]{1,0:T(8,128)(2,1)} %param.10), kind=kLoop, calls=%fused_computation.12 | loop fusion | flops 5242880 | bytes 6291456 | tf_op jit(solution)/shard_map/jit(silu)/mul | solution.py:67
  29.2 0.8 fusion.63
  30.0 5.5 %copy.53 = f32[512,2048]{0,1:T(8,128)} copy(f32[512,2048]{1,0:T(8,128)} %convert_multiply_fusion) | data formatting | bytes 8388608 | tf_op jit(solution)/shard_map/jit(silu)/mul | solution.py:67
  35.9 1.7 %collective-permute-start.3 = (bf16[512,64]{1,0:T(8,128)(2,1)S(1)}, bf16[512,64]{1,0:T(8,128)(2,1)S(1)}, u32[]{:S(2)}, u32[]{:S(2)}) collective-permute-start(bf16[512,64]{1,0:T(8,128)(2,1)S(1)} %multiply_convert_fusion.1), channel_id=1, source_target_pairs={{0,3},{1,0},{2,1},{3,2},{4,7},{5,4},{6,5},{7,6},{8,11},{9,8},{10,9... | collective-permute-start | bytes 196616 | tf_op jit(solution)/shard_map/ppermute | solution.py:20
  37.7 4.2 %divide_multiply_fusion = f32[512,2048]{1,0:T(8,128)S(1)} fusion(bf16[512,2048]{1,0:T(8,128)(2,1)S(1)} %copy-done.2, bf16[3,2048]{1,0:T(4,128)(2,1)S(1)} %collective-permute-done.4, f32[2048]{0:T(1024)S(1)} %bitcast.140, f32[2048]{0:T(1024)S(1)} %bitcast.141, f32[2048]{0:T(1024)S(1)} %bitcast.139, f32[2048]{0:T(1024)S(1)} %bitcast.138, ...), kind=kLoop, calls=%fused_computation.25 | loop fusion | flops 28311552 | bytes 6338048 | tf_op jit(solution)/shard_map/jit(silu)/mul | solution.py:39
  41.9 1.7 %fusion.79 = (f32[256,2048]{1,0:T(8,128)}, f32[256,2048]{1,0:T(8,128)S(1)}) fusion(f32[512,2048]{1,0:T(8,128)S(1)} %divide_multiply_fusion), kind=kLoop, calls=%fused_computation.138 | loop fusion | bytes 8388608 | tf_op jit(solution)/shard_map/slice | solution.py:100
  43.6 1.9 %copy.50 = f32[256,2048]{0,1:T(8,128)} copy(f32[256,2048]{1,0:T(8,128)S(1)} %get-tuple-element.20) | data formatting | bytes 4194304 | tf_op jit(solution)/shard_map/slice | solution.py:100
  45.5 1.9 %copy.47 = f32[256,2048]{0,1:T(8,128)S(1)} copy(f32[256,2048]{1,0:T(8,128)} %get-tuple-element.18) | data formatting | bytes 4194304 | tf_op jit(solution)/shard_map/slice | solution.py:100
  47.9 1.9 %fusion.33 = f32[32,64,128]{2,1,0:T(8,128)S(1)} fusion(f32[256,32,64]{0,2,1:T(8,128)S(1)} %bitcast.131, f32[256,32]{0,1:T(8,128)S(1)} %exponential_select_fusion.1, f32[32]{0:T(128)} %fusion.71, bf16[512,512]{1,0:T(8,128)(2,1)S(1)} %concatenate.20, s32[]{:T(128)S(6)} %select_n.116), kind=kOutput, calls=%fused_computation.44 | convolution fusion | flops 806092800 | bytes 3244164 | tf_op jit(solution)/shard_map/sh,shp,sn->hpn/dot_general | solution.py:60
  49.8 1.9 %add_add_fusion = f32[32,64,128]{2,1,0:T(8,128)S(1)} fusion(f32[32,64,128]{2,1,0:T(8,128)S(1)} %fusion.33, f32[32]{0:T(128)} %broadcast_select_fusion, f32[32]{0:T(128)} %fusion.63, f32[256,32,64]{0,2,1:T(8,128)S(1)} %bitcast.133, f32[256,32]{0,1:T(8,128)S(1)} %exponential_select_fusion, bf16[512,512]{1,0:T(8,128)(2,1)S(1)} %concatenate.20, s32[]{:T(128)S(6)} %add.101, ...), kind=kOutput, calls=%fused_computation.45 | convolution fusion | flops 806617088 | bytes 4292872 | tf_op jit(solution)/shard_map/sh,shp,sn->hpn/dot_general | solution.py:60
  51.7 1.8 %collective-permute-start.5 = (f32[32,64,128]{2,1,0:T(8,128)S(1)}, f32[32,64,128]{2,1,0:T(8,128)S(1)}, u32[]{:S(2)}, u32[]{:S(2)}) collective-permute-start(f32[32,64,128]{2,1,0:T(8,128)S(1)} %add_add_fusion), channel_id=1, source_target_pairs={{0,4},{4,8},{8,12},{12,16},{16,20},{20,24},{24,28},{28,0},{1,5},{5... | collective-permute-start | bytes 3145736 | tf_op jit(solution)/shard_map/while/body/eval_jaxpr/ppermute | solution.py:28
  53.8 9.9 %fusion.6 = f32[32,256,64]{1,2,0:T(8,128)S(1)} fusion(f32[256,32,64]{0,2,1:T(8,128)S(1)} %bitcast.132, f32[256,256]{1,0:T(8,128)S(1)} %fusion.52, f32[32,256]{1,0:T(8,128)S(1)} %get-tuple-element.25, pred[256,256]{1,0:T(8,128)(4,1)S(1)} %get-tuple-element.51), kind=kOutput, calls=%fused_computation.6 | convolution fusion | flops 1619001344 | bytes 4554752 | tf_op jit(solution)/shard_map/hts,shp->htp/dot_general | solution.py:54
  63.7 1.1 %bitcast_add_fusion.1 = f32[32,256,64]{1,2,0:T(8,128)S(1)} fusion(f32[32,256,64]{1,2,0:T(8,128)S(1)} %fusion.6, f32[32,256]{1,0:T(8,128)S(1)} %fusion.75, pred[256]{0:T(512)(128)(4,1)S(1)} %copy-done.6, bf16[512,512]{1,0:T(8,128)(2,1)S(1)} %concatenate.20, s32[]{:T(128)S(6)} %add.100), kind=kOutput, calls=%fused_computation.39 | convolution fusion | flops 806879232 | bytes 4293124 | tf_op jit(solution)/shard_map/tn,hpn->htp/dot_general | solution.py:56
  65.1 10.2 %fusion = f32[32,256,64]{1,2,0:T(8,128)S(1)} fusion(f32[256,32,64]{0,2,1:T(8,128)S(1)} %bitcast.134, f32[256,256]{1,0:T(8,128)S(1)} %fusion.57, f32[32,256]{1,0:T(8,128)S(1)} %get-tuple-element.24, pred[256,256]{1,0:T(8,128)(4,1)S(1)} %get-tuple-element.50), kind=kOutput, calls=%fused_computation | convolution fusion | flops 1619001344 | bytes 4554752 | tf_op jit(solution)/shard_map/hts,shp->htp/dot_general | solution.py:54
  75.3 1.1 %bitcast_add_fusion = f32[32,256,64]{1,2,0:T(8,128)S(1)} fusion(f32[32,256,64]{1,2,0:T(8,128)S(1)} %fusion, f32[32,64,128]{2,1,0:T(8,128)S(1)} %fusion.33, f32[32,256]{1,0:T(8,128)S(1)} %fusion.77, pred[256]{0:T(512)(128)(4,1)S(1)} %copy-done.5, bf16[512,512]{1,0:T(8,128)(2,1)S(1)} %concatenate.20, s32[]{:T(128)S(6)} %add.101, s32[]{:T(128)S(6)} %add.100), kind=kOutput, calls=%fused_computation.38 | convolution fusion | flops 806879232 | bytes 5341704 | tf_op jit(solution)/shard_map/tn,hpn->htp/dot_general | solution.py:56
  76.4 3.7 %collective-permute-done.5 = f32[32,64,128]{2,1,0:T(8,128)S(1)} collective-permute-done((f32[32,64,128]{2,1,0:T(8,128)S(1)}, f32[32,64,128]{2,1,0:T(8,128)S(1)}, u32[]{:S(2)}, u32[]{:S(2)}) %collective-permute-start.5) | collective-permute-done | bytes 1048608 | tf_op jit(solution)/shard_map/while/body/eval_jaxpr/ppermute | solution.py:28
  80.1 2.6 %multiply_reduce_fusion = (f32[512,32]{0,1:T(8,128)S(1)}, f32[512,32,64]{0,2,1:T(8,128)S(1)}) fusion(f32[512,32,64]{0,2,1:T(8,128)S(1)} %bitcast.129, f32[32,64,128]{2,1,0:T(8,128)S(1)} %collective-permute-done.5, bf16[512,512]{1,0:T(8,128)(2,1)S(1)} %concatenate.20, s32[]{:T(128)S(6)} %add.100, f32[32,512]{1,0:T(8,128)S(1)} %bitcast_exponential_fusion, ...), kind=kOutput, calls=%fused_computation.21 | convolution fusion | flops 1617936384 | bytes 13894148 | tf_op jit(solution)/shard_map/tn,hpn->htp/dot_general | solution.py:120
  83.3 2.4 %copy.54 = bf16[512,2048]{1,0:T(8,128)(2,1)} copy(bf16[512,2048]{0,1:T(8,128)(2,1)S(1)} %bitcast.130) | data formatting | bytes 4194304 | tf_op jit(solution)/shard_map/convert_element_type | solution.py:70
  (61 shorter events, 7.6 us)
Async XLA Ops:
  4.1 31.4 %collective-permute-start = (bf16[3,64]{1,0:T(4,128)(2,1)S(1)}, bf16[3,64]{1,0:T(4,128)(2,1)S(1)}, u32[]{:S(2)}, u32[]{:S(2)}) collective-permute-start(bf16[3,64]{1,0:T(4,128)(2,1)S(1)} %slice_select_fusion.1), channel_id=1, source_target_pairs={{0,4},{4,8},{8,12},{12,16},{16,20},{20,24},{24,28},{28,0},{1,5},{5... | collective-permute-start | bytes 1160 | tf_op jit(solution)/shard_map/ppermute | solution.py:28
  7.9 29.7 %collective-permute-start.4 = (bf16[3,2048]{1,0:T(4,128)(2,1)S(1)}, bf16[3,2048]{1,0:T(4,128)(2,1)S(1)}, u32[]{:S(2)}, u32[]{:S(2)}) collective-permute-start(bf16[3,2048]{1,0:T(4,128)(2,1)S(1)} %slice_select_fusion), channel_id=1, source_target_pairs={{0,4},{4,8},{8,12},{12,16},{16,20},{20,24},{24,28},{28,0},{1,5},{5... | collective-permute-start | bytes 36872 | tf_op jit(solution)/shard_map/ppermute | solution.py:28
  30.0 5.5 %copy-start.3 = (bf16[2048]{0:T(1024)(128)(2,1)S(1)}, bf16[2048]{0:T(1024)(128)(2,1)}, u32[]{:S(2)}) copy-start(bf16[2048]{0:T(1024)(128)(2,1)} %param.16) | copy-start | bytes 12292
  30.0 7.7 %copy-start.2 = (bf16[512,2048]{1,0:T(8,128)(2,1)S(1)}, bf16[512,2048]{1,0:T(8,128)(2,1)}, u32[]{:S(2)}) copy-start(bf16[512,2048]{1,0:T(8,128)(2,1)} %param.9) | copy-start | bytes 6291460
  35.9 6.0 %collective-permute-start.1 = (bf16[512,64]{1,0:T(8,128)(2,1)S(1)}, bf16[512,64]{1,0:T(8,128)(2,1)S(1)}, u32[]{:S(2)}, u32[]{:S(2)}) collective-permute-start(bf16[512,64]{1,0:T(8,128)(2,1)S(1)} %multiply_convert_fusion.1), channel_id=1, source_target_pairs={{0,1},{1,2},{2,3},{3,0},{4,5},{5,6},{6,7},{7,4},{8,9},{9,10},{10,1... | collective-permute-start | bytes 196616 | tf_op jit(solution)/shard_map/ppermute | solution.py:18
  35.9 11.5 %collective-permute-start.3 = (bf16[512,64]{1,0:T(8,128)(2,1)S(1)}, bf16[512,64]{1,0:T(8,128)(2,1)S(1)}, u32[]{:S(2)}, u32[]{:S(2)}) collective-permute-start(bf16[512,64]{1,0:T(8,128)(2,1)S(1)} %multiply_convert_fusion.1), channel_id=1, source_target_pairs={{0,3},{1,0},{2,1},{3,2},{4,7},{5,4},{6,5},{7,6},{8,11},{9,8},{10,9... | collective-permute-start | bytes 196616 | tf_op jit(solution)/shard_map/ppermute | solution.py:20
  41.9 5.6 %collective-permute-start.2 = (bf16[512,64]{1,0:T(8,128)(2,1)S(1)}, bf16[512,64]{1,0:T(8,128)(2,1)S(1)}, u32[]{:S(2)}, u32[]{:S(2)}) collective-permute-start(bf16[512,64]{1,0:T(8,128)(2,1)S(1)} %collective-permute-done.1), channel_id=1, source_target_pairs={{0,1},{1,2},{2,3},{3,0},{4,5},{5,6},{6,7},{7,4},{8,9},{9,10},{10,1... | collective-permute-start | bytes 196616 | tf_op jit(solution)/shard_map/ppermute | solution.py:18
  47.9 1.9 %copy-start.1 = (f32[256,2048]{0,1:T(8,128)S(1)}, f32[256,2048]{0,1:T(8,128)}, u32[]{:S(2)}) copy-start(f32[256,2048]{0,1:T(8,128)} %copy.50) | copy-start | bytes 6291460
  51.7 28.4 %collective-permute-start.5 = (f32[32,64,128]{2,1,0:T(8,128)S(1)}, f32[32,64,128]{2,1,0:T(8,128)S(1)}, u32[]{:S(2)}, u32[]{:S(2)}) collective-permute-start(f32[32,64,128]{2,1,0:T(8,128)S(1)} %add_add_fusion), channel_id=1, source_target_pairs={{0,4},{4,8},{8,12},{12,16},{16,20},{20,24},{24,28},{28,0},{1,5},{5... | collective-permute-start | bytes 3145736 | tf_op jit(solution)/shard_map/while/body/eval_jaxpr/ppermute | solution.py:28
  53.8 9.9 %copy-start.6 = (pred[256]{0:T(512)(128)(4,1)S(1)}, pred[256]{0:T(512)(128)(4,1)}, u32[]{:S(2)}) copy-start(pred[256]{0:T(512)(128)(4,1)} %get-tuple-element.34) | copy-start | bytes 772
  65.1 10.2 %copy-start.5 = (pred[256]{0:T(512)(128)(4,1)S(1)}, pred[256]{0:T(512)(128)(4,1)}, u32[]{:S(2)}) copy-start(pred[256]{0:T(512)(128)(4,1)} %get-tuple-element.32) | copy-start | bytes 772
  75.3 4.8 %copy-start = (f32[512,2048]{0,1:T(8,128)S(1)}, f32[512,2048]{0,1:T(8,128)}, u32[]{:S(2)}) copy-start(f32[512,2048]{0,1:T(8,128)} %copy.53) | copy-start | bytes 12582916
  75.3 4.8 %copy-start.4 = (pred[512]{0:T(512)(128)(4,1)S(1)}, pred[512]{0:T(512)(128)(4,1)}, u32[]{:S(2)}) copy-start(pred[512]{0:T(512)(128)(4,1)} %get-tuple-element.11) | copy-start | bytes 1540
